TPU v7x, 256 devices: a whole 4x4x8 slice. The times are simulated.
256 devices in a mesh: ctx: 32 (over x, z), grp: 8 (over y, core).
Axes of the slice: x: 4, y: 4, z: 8, core: 2. Of those that a mesh axis runs over, the one named last changes fastest.
Arguments:
- out_grad: bfloat16 [16384, 2048], P('ctx', 'grp'), may hold values from -6 to 6
- filter_mats: bfloat16 [16, 2048, 2048], P('grp', 'ctx'), may hold values from -0.125 to 0.125
- coeffs: float32 [16, 80], replicated, may hold values from -0.15625 to 0.15625
- pole_rates: float32 [80], replicated, may hold values from 1.2207031e-06 to 0.03
Outputs:
- in_grad: bfloat16 [16384, 2048], P('ctx', 'grp')
All inputs are finite; a program needn't handle non-finite values.
Results may differ from a plain program's by a relative error of at most 0.001.
Values may be sent and summed in bfloat16 or wider, within the bound.
A program may use at most 128 MiB of HBM per device.

v0:
```python
import jax
import jax.numpy as jnp
from jax import lax
from jax.sharding import PartitionSpec as P

exact_prec = lax.Precision.HIGHEST


def entering(array, axis, combine, identity):
    count, here = (lax.axis_size(axis), lax.axis_index(axis))
    everything = jax.tree.map(lambda part: lax.all_gather(part, axis), array)
    start = jax.tree.map(
        lambda part, zero: jnp.broadcast_to(jnp.asarray(zero, part.dtype), part.shape),
        array,
        identity,
    )

    def step(k, before):
        at = count - 1 - k
        reached = at > here
        new = combine(before, jax.tree.map(lambda part: part[at], everything))
        return jax.tree.map(lambda a, b: jnp.where(reached, a, b), new, before)

    return lax.fori_loop(0, count, step, start)


def merge_suffix(earlier, latter):
    carried_e, factor_e = earlier
    carried_l, factor_l = latter
    return (carried_l + factor_l * carried_e, factor_l * factor_e)


def per_device(out_grad, filter_mats, coeffs, pole_rates):
    full_grad = lax.all_gather(out_grad, "grp", axis=1, tiled=True)
    length = full_grad.shape[0]
    col_width = out_grad.shape[1]
    poles = pole_rates.shape[0]
    positions = jnp.arange(length, dtype=jnp.float32)
    pole_gains = jnp.sqrt(-jnp.expm1(-2.0 * pole_rates))
    middle = float(length // 2)
    rising = jnp.exp(-(positions[:, None] - middle) * pole_rates[None, :])
    falling = jnp.exp((positions[:, None] - middle) * pole_rates[None, :])
    causal = positions[:, None] >= positions[None, :]
    decay_pos = jnp.exp(-positions[:, None] * pole_rates[None, :])
    edge_decay = pole_gains[None, :] * jnp.exp(-(length - positions)[:, None] * pole_rates[None, :])
    block_decay = jnp.exp(-length * pole_rates)[:, None]
    unit_factor = jnp.ones((poles, 1), jnp.float32)
    filters = filter_mats.shape[0]
    own_coeffs = lax.dynamic_slice_in_dim(coeffs, lax.axis_index("grp") * filters, filters, 0)
    kernel_mat = jnp.einsum(
        "tp,kp,sp->kts", rising, own_coeffs * pole_gains[None, :], falling, precision=exact_prec
    )
    kernel_mat = jnp.where(causal[None], kernel_mat, 0.0)
    weights = own_coeffs[:, :, None] * decay_pos.T[None]
    proj_grad = jnp.einsum(
        "tj,kij->kti",
        full_grad,
        lax.all_gather(filter_mats, "ctx", axis=1, tiled=True),
        preferred_element_type=jnp.float32,
    )
    near_part = jnp.einsum("kts,kti->si", kernel_mat, proj_grad, precision=exact_prec)
    pole_part = jnp.einsum("kpt,kti->pi", weights, proj_grad, precision=exact_prec)
    stacked = jnp.concatenate([near_part, pole_part], axis=0)
    near_sum = lax.psum_scatter(stacked[:length], "grp", scatter_dimension=1, tiled=True)
    pole_sum = lax.psum(stacked[length:], "grp")
    later_all = entering(
        (pole_sum, block_decay), "ctx", merge_suffix, (jnp.zeros_like(pole_sum), unit_factor)
    )[0]
    own_cols = lax.dynamic_slice_in_dim(later_all, lax.axis_index("grp") * col_width, col_width, 1)
    total = near_sum + jnp.dot(edge_decay, own_cols, precision=exact_prec)
    return total.astype(jnp.bfloat16)


def solution(mesh):
    placed = (P("ctx", "grp"), P("grp", "ctx", None), P(), P())
    return jax.shard_map(
        per_device, mesh=mesh, in_specs=placed, out_specs=P("ctx", "grp"), check_vma=False
    )
```

profile of v0, /device:TPU:0, one launch (start us, length us, event | category | flops | bytes accessed | tf_op | source)
XLA Modules:
  0.0 490.5 jit_solution(5679977234924721466)
XLA Ops:
  8.1 1.3 dynamic-slice
  12.2 27.7 %all-gather.7.cloned.1.call-done = bf16[512,2048]{1,0:T(8,128)(2,1)} async-done(((bf16[512,256]{1,0:T(8,128)(2,1)}), bf16[512,2048]{1,0:T(8,128)(2,1)}) %all-gather.7.cloned.1.call-update) | async-done | bytes 2097168 | tf_op jit(solution)/shard_map/all_gather | solution.py:34
  39.9 143.1 %all-gather.5.cloned.1.call-done = bf16[2,2048,2048]{2,1,0:T(8,128)(2,1)} async-done(((bf16[2,64,2048]{2,1,0:T(8,128)(2,1)}), bf16[2,2048,2048]{2,1,0:T(8,128)(2,1)}) %all-gather.5.cloned.1.call-update) | async-done | bytes 16777232 | tf_op jit(solution)/shard_map/all_gather | solution.py:58
  183.0 12.9 %fusion.11 = f32[2,2048,512]{2,1,0:T(8,128)S(1)} fusion(bf16[2,2048,2048]{2,1,0:T(8,128)(2,1)} %all-gather.5.cloned.1.call-done, bf16[512,2048]{1,0:T(8,128)(2,1)} %all-gather.7.cloned.1.call-done), kind=kOutput, calls=%fused_computation.9 | convolution fusion | flops 8589934592 | bytes 27262976 | tf_op jit(solution)/shard_map/tj,kij->kti/dot_general | solution.py:55
  195.9 3.3 copy-done
  199.2 9.1 %fusion.8 = f32[1,80,2048]{2,1,0:T(8,128)} fusion(f32[2,2048,512]{2,1,0:T(8,128)S(1)} %fusion.11, f32[80,512]{1,0:T(8,128)S(1)} %multiply_exponential_fusion, f32[2,80]{1,0:T(2,128)S(1)} %get-tuple-element.167), kind=kOutput, calls=%fused_computation.8 | convolution fusion | flops 2013347840 | bytes 9208448 | tf_op jit(solution)/shard_map/kpt,kti->pi/dot_general | solution.py:62
  208.3 63.9 %all-reduce.3.cloned.1.call-done = f32[1,80,2048]{2,1,0:T(8,128)} async-done(((f32[1,80,2048]{2,1,0:T(8,128)}), f32[1,80,2048]{2,1,0:T(8,128)}) %all-reduce.3.cloned.1.call-update) | async-done | bytes 655376 | tf_op jit(solution)/shard_map/psum | solution.py:65
  272.4 147.7 %all-reduce = f32[2560]{0:T(1024)S(1)} all-reduce(f32[2560]{0:T(1024)S(1)} %get-tuple-element.168), channel_id=2, replica_groups=mesh['ctx'=32,'grp'=8] {'ctx'}, use_global_device_ids=true, to_apply=%add | all-reduce | flops 2560 | bytes 20480
  420.7 1.9 fusion.17
  422.6 17.5 %fusion.5 = f32[512,2048]{1,0:T(8,128)} fusion(f32[2,2048,512]{2,1,0:T(8,128)} %copy-done, f32[2,512,512]{1,2,0:T(8,128)S(1)} %fusion.17, pred[512,512]{0,1:T(8,128)(4,1)S(1)} %iota_compare_fusion), kind=kOutput, calls=%fused_computation.7 | convolution fusion | flops 12885426176 | bytes 14942208 | tf_op jit(solution)/shard_map/kts,kti->si/dot_general | solution.py:61
  440.1 41.4 %while.16 = (s32[]{:T(128)}, f32[80,2048]{1,0:T(8,128)S(1)}, s32[]{:T(128)}, f32[32,80,2048]{2,1,0:T(8,128)}, f32[32,80,1]{1,2,0:T(1,128)S(1)}, /*index=5*/s32[]{:T(128)}, s32[]{:T(128)}, s32[]{:T(128)}, s32[]{:T(128)}) while((s32[]{:T(128)}, f32[80,2048]{1,0:T(8,128)S(1)}, s32[]{:T(128)}, f32[32,80,2048]{2,1,0:T(8,128)}, ...), condition=%wide.region_3.4_spmd.clone, body=%wide.region_2.3_spmd.clone.sunk | while | flops 655368 | bytes 1967215 | solution.py:24
  445.3 1.2 fusion.39
  446.6 1.3 fusion.39
  450.5 1.2 fusion.39
  451.8 1.3 fusion.39
  453.1 1.2 fusion.39
  454.4 1.2 fusion.39
  455.7 1.2 fusion.39
  458.3 1.2 fusion.39
  459.6 1.2 fusion.39
  460.8 1.2 fusion.39
  462.1 1.3 fusion.39
  463.4 1.2 fusion.39
  466.0 1.3 fusion.39
  467.3 1.3 fusion.39
  468.6 1.2 fusion.39
  469.9 1.2 fusion.39
  472.5 1.2 fusion.39
  473.8 1.2 fusion.39
  475.1 1.2 fusion.39
  479.0 1.2 fusion.39
  481.5 2.5 fusion.14
  (73 shorter events, 19.7 us)
Async XLA Ops:
  6.5 33.4 %all-gather.7.cloned.1.call-start = ((), (), s32[]{:S(2)}) async-start(), calls=%async_computation.2 | async-start | bytes 2359296 | tf_op jit(solution)/shard_map/all_gather | solution.py:34
  7.3 175.8 %all-gather.5.cloned.1.call-start = ((), (), s32[]{:S(2)}) async-start(), calls=%async_computation.1 | async-start | bytes 17301504 | tf_op jit(solution)/shard_map/all_gather | solution.py:58
  8.0 264.2 %all-reduce.3.cloned.1.call-start = ((), (), s32[]{:S(2)}) async-start(), calls=%async_computation.4 | async-start | bytes 1310720 | tf_op jit(solution)/shard_map/psum | solution.py:65
  195.9 3.3 copy-start
  195.9 224.5 %copy-start.1 = (f32[80]{0:T(128)S(1)}, f32[80]{0:T(128)}, u32[]{:S(2)}) copy-start(f32[80]{0:T(128)} %param.9) | copy-start | bytes 964
  208.3 231.8 %all-gather.9.cloned.1.call-start = ((), (), s32[]{:S(2)}) async-start(), calls=%async_computation.5 | async-start | bytes 21626880 | tf_op jit(solution)/shard_map/all_gather | solution.py:11
  272.2 209.3 %reduce-scatter.2.cloned.1.call-start = ((), (), s32[]{:S(2)}) async-start(), calls=%async_computation.3 | async-start | bytes 4718592 | tf_op jit(solution)/shard_map/reduce_scatter | solution.py:64
Sparse Core Ops, SparseCore 0:
  9.2 30.7 all-gather.6
  42.5 140.4 all-gather.4
  208.4 63.7 all-reduce.2
  274.6 161.0 all-gather.8
  440.2 35.2 reduce-scatter.1
where the time goes:
time: 492 us; the launch traced here: 491 us
  waiting for transfers between devices  236 us (48%)
  blocking collectives  148 us (30%)
  matrix products  43.8 us (9%)
  other arithmetic  42.5 us (9%)
  between operations  13.9 us (3%)
  local copies, waits for them, and re-layouts  4.96 us (1%)
    unnamed x1, blocking collectives  148 us
    all_gather x1, waiting for transfers between devices, per_device(): lax.all_gather(filter_mats, 'ctx', axis=1, tiled=True)  143 us
    psum x1, waiting for transfers between devices, per_device(): pole_sum = lax.psum(stacked[length:], 'grp')  63.9 us
    select_n x32, other arithmetic, step(): return jax.tree.map(lambda a, b: jnp.where(reached, a, b), new, before)  39.8 us
    all_gather x1, waiting for transfers between devices, per_device(): full_grad = lax.all_gather(out_grad, 'grp', axis=1, tiled=True)  27.7 us
    dot_general x1, matrix products, per_device(): jnp.einsum('kts,kti->si', kernel_mat, proj_grad, precision=exact_prec)  17.5 us
    dot_general x1, matrix products, per_device(): jnp.einsum('tj,kij->kti', full_grad, lax.all_gather(filter_mats, 'ctx', a...  12.9 us
  transfers between devices with their start and end apart: 5, of which 3 were waited for; matrix products, arithmetic and copies ran while one was open for 13% of the time, Pallas kernels for 0%

commit v1 on v0

--- a/solution.py
+++ b/solution.py
@@ -31,7 +31,12 @@
 
 
 def per_device(out_grad, filter_mats, coeffs, pole_rates):
-    full_grad = lax.all_gather(out_grad, "grp", axis=1, tiled=True)
+    ring = [out_grad]
+    for hop in range(7):
+        ring.append(lax.ppermute(ring[-1], "grp", [(dev, (dev + 1) % 8) for dev in range(8)]))
+    full_grad = jnp.roll(
+        jnp.concatenate(ring[::-1], axis=1), (lax.axis_index("grp") + 1) * ring[0].shape[1], axis=1
+    )
     length = full_grad.shape[0]
     col_width = out_grad.shape[1]
     poles = pole_rates.shape[0]

time: 492 us -> 457 us (0.929)
  waiting for transfers between devices: 236 us -> 192 us
  local copies, waits for them, and re-layouts: 4.96 us -> 17 us
    all_gather x1, waiting for transfers between devices: 143 us -> 82.2 us  [per_device(): lax.all_gather(filter_mats, 'ctx', axis=1, tiled=True)]
    ppermute x0 -> x7, waiting for transfers between devices: none -> 45.1 us  [per_device(): lax.ppermute(ring[-1], 'grp', [(dev, (dev + 1) % 8) for dev in range(8)])]
    all_gather x1 -> x0, waiting for transfers between devices: 27.7 us -> none  [per_device(): full_grad = lax.all_gather(out_grad, 'grp', axis=1, tiled=True)]
    unnamed x6 -> x23, local copies, waits for them, and re-layouts: 4.53 us -> 15.8 us
  transfers between devices with their start and end apart: 5 -> 11, of which waited for: 3 -> 9; matrix products, arithmetic and copies ran while one was open for 13% -> 17% of each run, Pallas kernels for 0% -> 0%
where the time goes in v1:
time: 457 us; the launch traced here: 455 us
  waiting for transfers between devices  192 us (42%)
  blocking collectives  148 us (32%)
  other arithmetic  42.5 us (9%)
  matrix products  40.3 us (9%)
  local copies, waits for them, and re-layouts  17 us (4%)
  between operations  13.9 us (3%)
    unnamed x1, blocking collectives  148 us
    all_gather x1, waiting for transfers between devices, per_device(): lax.all_gather(filter_mats, 'ctx', axis=1, tiled=True)  82.2 us
    psum x1, waiting for transfers between devices, per_device(): pole_sum = lax.psum(stacked[length:], 'grp')  63.9 us
    ppermute x7, waiting for transfers between devices, per_device(): lax.ppermute(ring[-1], 'grp', [(dev, (dev + 1) % 8) for dev in range(8)])  45.1 us
    select_n x32, other arithmetic, step(): return jax.tree.map(lambda a, b: jnp.where(reached, a, b), new, before)  39.8 us
    dot_general x1, matrix products, per_device(): jnp.einsum('kts,kti->si', kernel_mat, proj_grad, precision=exact_prec)  17.5 us
    unnamed x23, local copies, waits for them, and re-layouts  15.8 us
    dot_general x1, matrix products, per_device(): jnp.einsum('tj,kij->kti', full_grad, lax.all_gather(filter_mats, 'ctx', a...  12.4 us
  transfers between devices with their start and end apart: 11, of which 9 were waited for; matrix products, arithmetic and copies ran while one was open for 17% of the time, Pallas kernels for 0%

profile of v1, /device:TPU:0, one launch (start us, length us, event | category | flops | bytes accessed | tf_op | source)
XLA Modules:
  0.0 454.8 jit_solution(15140991876417399688)
XLA Ops:
  7.3 7.2 %collective-permute-done = bf16[512,256]{1,0:T(8,128)(2,1)S(1)} collective-permute-done((bf16[512,256]{1,0:T(8,128)(2,1)}, bf16[512,256]{1,0:T(8,128)(2,1)S(1)}, u32[]{:S(2)}, u32[]{:S(2)}) %collective-permute-start) | collective-permute-done | bytes 262176 | tf_op jit(solution)/shard_map/ppermute | solution.py:36
  14.5 7.0 %collective-permute-done.1 = bf16[512,256]{1,0:T(8,128)(2,1)S(1)} collective-permute-done((bf16[512,256]{1,0:T(8,128)(2,1)S(1)}, bf16[512,256]{1,0:T(8,128)(2,1)S(1)}, u32[]{:S(2)}, u32[]{:S(2)}) %collective-permute-start.1) | collective-permute-done | bytes 262176 | tf_op jit(solution)/shard_map/ppermute | solution.py:36
  21.5 7.0 %collective-permute-done.2 = bf16[512,256]{1,0:T(8,128)(2,1)S(1)} collective-permute-done((bf16[512,256]{1,0:T(8,128)(2,1)S(1)}, bf16[512,256]{1,0:T(8,128)(2,1)S(1)}, u32[]{:S(2)}, u32[]{:S(2)}) %collective-permute-start.2) | collective-permute-done | bytes 262176 | tf_op jit(solution)/shard_map/ppermute | solution.py:36
  28.6 7.0 %collective-permute-done.3 = bf16[512,256]{1,0:T(8,128)(2,1)S(1)} collective-permute-done((bf16[512,256]{1,0:T(8,128)(2,1)S(1)}, bf16[512,256]{1,0:T(8,128)(2,1)S(1)}, u32[]{:S(2)}, u32[]{:S(2)}) %collective-permute-start.3) | collective-permute-done | bytes 262176 | tf_op jit(solution)/shard_map/ppermute | solution.py:36
  35.6 1.3 dynamic-slice
  37.5 5.1 %collective-permute-done.4 = bf16[512,256]{1,0:T(8,128)(2,1)S(1)} collective-permute-done((bf16[512,256]{1,0:T(8,128)(2,1)S(1)}, bf16[512,256]{1,0:T(8,128)(2,1)S(1)}, u32[]{:S(2)}, u32[]{:S(2)}) %collective-permute-start.4) | collective-permute-done | bytes 262176 | tf_op jit(solution)/shard_map/ppermute | solution.py:36
  44.0 5.6 %collective-permute-done.5 = bf16[512,256]{1,0:T(8,128)(2,1)S(1)} collective-permute-done((bf16[512,256]{1,0:T(8,128)(2,1)S(1)}, bf16[512,256]{1,0:T(8,128)(2,1)S(1)}, u32[]{:S(2)}, u32[]{:S(2)}) %collective-permute-start.5) | collective-permute-done | bytes 262176 | tf_op jit(solution)/shard_map/ppermute | solution.py:36
  50.4 6.2 %collective-permute-done.6 = bf16[512,256]{1,0:T(8,128)(2,1)S(1)} collective-permute-done((bf16[512,256]{1,0:T(8,128)(2,1)S(1)}, bf16[512,256]{1,0:T(8,128)(2,1)S(1)}, u32[]{:S(2)}, u32[]{:S(2)}) %collective-permute-start.6) | collective-permute-done | bytes 262176 | tf_op jit(solution)/shard_map/ppermute | solution.py:36
  68.6 82.2 %all-gather.4.cloned.1.call-done = bf16[2,2048,2048]{2,1,0:T(8,128)(2,1)} async-done(((bf16[2,64,2048]{2,1,0:T(8,128)(2,1)}), bf16[2,2048,2048]{2,1,0:T(8,128)(2,1)}) %all-gather.4.cloned.1.call-update) | async-done | bytes 16777232 | tf_op jit(solution)/shard_map/all_gather | solution.py:63
  150.9 12.4 %fusion.11 = f32[512,2,2048]{2,0,1:T(8,128)S(1)} fusion(bf16[2,2048,2048]{2,1,0:T(8,128)(2,1)} %all-gather.4.cloned.1.call-done, bf16[512,4096]{1,0:T(8,128)(2,1)} %constant_dynamic-update-slice_fusion, s32[]{:T(128)S(6)} %select_n.59), kind=kOutput, calls=%fused_computation.9 | convolution fusion | flops 8589934592 | bytes 27262980 | tf_op jit(solution)/shard_map/tj,kij->kti/dot_general | solution.py:60
  163.3 3.3 copy-done
  166.5 6.0 %fusion.8 = f32[1,80,2048]{2,1,0:T(8,128)} fusion(f32[512,2,2048]{2,0,1:T(8,128)S(1)} %fusion.11, f32[80,512]{1,0:T(8,128)S(1)} %multiply_exponential_fusion, f32[2,80]{1,0:T(2,128)S(1)} %get-tuple-element.167), kind=kOutput, calls=%fused_computation.8 | convolution fusion | flops 2013347840 | bytes 9208448 | tf_op jit(solution)/shard_map/kpt,kti->pi/dot_general | solution.py:67
  172.6 63.9 %all-reduce.3.cloned.1.call-done = f32[1,80,2048]{2,1,0:T(8,128)} async-done(((f32[1,80,2048]{2,1,0:T(8,128)}), f32[1,80,2048]{2,1,0:T(8,128)}) %all-reduce.3.cloned.1.call-update) | async-done | bytes 655376 | tf_op jit(solution)/shard_map/psum | solution.py:70
  236.7 147.6 %all-reduce = f32[2560]{0:T(1024)S(1)} all-reduce(f32[2560]{0:T(1024)S(1)} %get-tuple-element.168), channel_id=2, replica_groups=mesh['ctx'=32,'grp'=8] {'ctx'}, use_global_device_ids=true, to_apply=%add | all-reduce | flops 2560 | bytes 20480
  384.9 1.9 fusion.18
  386.9 17.5 %fusion.5 = f32[512,2048]{1,0:T(8,128)} fusion(f32[512,2,2048]{2,0,1:T(8,128)} %copy-done, f32[2,512,512]{1,2,0:T(8,128)S(1)} %fusion.18, pred[512,512]{0,1:T(8,128)(4,1)S(1)} %iota_compare_fusion), kind=kOutput, calls=%fused_computation.7 | convolution fusion | flops 12885426176 | bytes 14942208 | tf_op jit(solution)/shard_map/kts,kti->si/dot_general | solution.py:66
  404.4 41.4 %while.16 = (s32[]{:T(128)}, f32[80,2048]{1,0:T(8,128)S(1)}, s32[]{:T(128)}, f32[32,80,2048]{2,1,0:T(8,128)}, f32[32,80,1]{1,2,0:T(1,128)S(1)}, /*index=5*/s32[]{:T(128)}, s32[]{:T(128)}, s32[]{:T(128)}, s32[]{:T(128)}) while((s32[]{:T(128)}, f32[80,2048]{1,0:T(8,128)S(1)}, s32[]{:T(128)}, f32[32,80,2048]{2,1,0:T(8,128)}, ...), condition=%wide.region_3.4_spmd.clone, body=%wide.region_2.3_spmd.clone.sunk | while | flops 655368 | bytes 1967207 | solution.py:24
  410.9 1.3 fusion.41
  414.8 1.2 fusion.41
  416.1 1.3 fusion.41
  417.4 1.2 fusion.41
  418.7 1.2 fusion.41
  420.0 1.2 fusion.41
  422.6 1.2 fusion.41
  423.9 1.2 fusion.41
  425.2 1.3 fusion.41
  426.5 1.3 fusion.41
  430.4 1.3 fusion.41
  431.7 1.3 fusion.41
  433.0 1.2 fusion.41
  439.4 1.2 fusion.41
  445.9 2.5 fusion.15
  (102 shorter events, 38.4 us)
Async XLA Ops:
  6.5 55.3 %copy-start.1 = (bf16[512,256]{1,0:T(8,128)(2,1)S(1)}, bf16[512,256]{1,0:T(8,128)(2,1)}, u32[]{:S(2)}) copy-start(bf16[512,256]{1,0:T(8,128)(2,1)} %param.6) | copy-start | bytes 786436
  6.5 144.3 %all-gather.4.cloned.1.call-start = ((), (), s32[]{:S(2)}) async-start(), calls=%async_computation.1 | async-start | bytes 17301504 | tf_op jit(solution)/shard_map/all_gather | solution.py:63
  7.3 229.3 %all-reduce.3.cloned.1.call-start = ((), (), s32[]{:S(2)}) async-start(), calls=%async_computation.3 | async-start | bytes 1310720 | tf_op jit(solution)/shard_map/psum | solution.py:70
  7.3 7.2 %collective-permute-start = (bf16[512,256]{1,0:T(8,128)(2,1)}, bf16[512,256]{1,0:T(8,128)(2,1)S(1)}, u32[]{:S(2)}, u32[]{:S(2)}) collective-permute-start(bf16[512,256]{1,0:T(8,128)(2,1)} %param.6), channel_id=1, source_target_pairs={{0,1},{1,2},{2,3},{3,4},{4,5},{5,6},{6,7},{7,0},{8,9},{9,10},{10,1... | collective-permute-start | bytes 786440 | tf_op jit(solution)/shard_map/ppermute | solution.py:36
  14.5 7.0 %collective-permute-start.1 = (bf16[512,256]{1,0:T(8,128)(2,1)S(1)}, bf16[512,256]{1,0:T(8,128)(2,1)S(1)}, u32[]{:S(2)}, u32[]{:S(2)}) collective-permute-start(bf16[512,256]{1,0:T(8,128)(2,1)S(1)} %collective-permute-done), channel_id=1, source_target_pairs={{0,1},{1,2},{2,3},{3,4},{4,5},{5,6},{6,7},{7,0},{8,9},{9,10},{10,1... | collective-permute-start | bytes 786440 | tf_op jit(solution)/shard_map/ppermute | solution.py:36
  21.5 7.0 %collective-permute-start.2 = (bf16[512,256]{1,0:T(8,128)(2,1)S(1)}, bf16[512,256]{1,0:T(8,128)(2,1)S(1)}, u32[]{:S(2)}, u32[]{:S(2)}) collective-permute-start(bf16[512,256]{1,0:T(8,128)(2,1)S(1)} %collective-permute-done.1), channel_id=1, source_target_pairs={{0,1},{1,2},{2,3},{3,4},{4,5},{5,6},{6,7},{7,0},{8,9},{9,10},{10,1... | collective-permute-start | bytes 786440 | tf_op jit(solution)/shard_map/ppermute | solution.py:36
  28.6 7.0 %collective-permute-start.3 = (bf16[512,256]{1,0:T(8,128)(2,1)S(1)}, bf16[512,256]{1,0:T(8,128)(2,1)S(1)}, u32[]{:S(2)}, u32[]{:S(2)}) collective-permute-start(bf16[512,256]{1,0:T(8,128)(2,1)S(1)} %collective-permute-done.2), channel_id=1, source_target_pairs={{0,1},{1,2},{2,3},{3,4},{4,5},{5,6},{6,7},{7,0},{8,9},{9,10},{10,1... | collective-permute-start | bytes 786440 | tf_op jit(solution)/shard_map/ppermute | solution.py:36
  35.6 7.0 %collective-permute-start.4 = (bf16[512,256]{1,0:T(8,128)(2,1)S(1)}, bf16[512,256]{1,0:T(8,128)(2,1)S(1)}, u32[]{:S(2)}, u32[]{:S(2)}) collective-permute-start(bf16[512,256]{1,0:T(8,128)(2,1)S(1)} %collective-permute-done.3), channel_id=1, source_target_pairs={{0,1},{1,2},{2,3},{3,4},{4,5},{5,6},{6,7},{7,0},{8,9},{9,10},{10,1... | collective-permute-start | bytes 786440 | tf_op jit(solution)/shard_map/ppermute | solution.py:36
  42.6 7.0 %collective-permute-start.5 = (bf16[512,256]{1,0:T(8,128)(2,1)S(1)}, bf16[512,256]{1,0:T(8,128)(2,1)S(1)}, u32[]{:S(2)}, u32[]{:S(2)}) collective-permute-start(bf16[512,256]{1,0:T(8,128)(2,1)S(1)} %collective-permute-done.4), channel_id=1, source_target_pairs={{0,1},{1,2},{2,3},{3,4},{4,5},{5,6},{6,7},{7,0},{8,9},{9,10},{10,1... | collective-permute-start | bytes 786440 | tf_op jit(solution)/shard_map/ppermute | solution.py:36
  49.6 7.0 %collective-permute-start.6 = (bf16[512,256]{1,0:T(8,128)(2,1)S(1)}, bf16[512,256]{1,0:T(8,128)(2,1)S(1)}, u32[]{:S(2)}, u32[]{:S(2)}) collective-permute-start(bf16[512,256]{1,0:T(8,128)(2,1)S(1)} %collective-permute-done.5), channel_id=1, source_target_pairs={{0,1},{1,2},{2,3},{3,4},{4,5},{5,6},{6,7},{7,0},{8,9},{9,10},{10,1... | collective-permute-start | bytes 786440 | tf_op jit(solution)/shard_map/ppermute | solution.py:36
  163.3 3.3 copy-start
  166.5 218.1 %copy-start.2 = (f32[80]{0:T(128)S(1)}, f32[80]{0:T(128)}, u32[]{:S(2)}) copy-start(f32[80]{0:T(128)} %param.9) | copy-start | bytes 964
  172.6 231.8 %all-gather.6.cloned.1.call-start = ((), (), s32[]{:S(2)}) async-start(), calls=%async_computation.4 | async-start | bytes 21626880 | tf_op jit(solution)/shard_map/all_gather | solution.py:11
  236.5 209.3 %reduce-scatter.2.cloned.1.call-start = ((), (), s32[]{:S(2)}) async-start(), calls=%async_computation.2 | async-start | bytes 4718592 | tf_op jit(solution)/shard_map/reduce_scatter | solution.py:69
Sparse Core Ops, SparseCore 0:
  9.9 140.8 all-gather.3
  172.7 63.7 all-reduce.2
  239.1 161.0 all-gather.5
  404.5 35.4 reduce-scatter.1
